TPU v7x, 256 devices: a whole 4x4x8 slice. The times are simulated.
256 devices in a mesh: axial: 16 (over x, z_hi, core), radial: 4 (over y), pitch: 4 (over z_lo).
Axes of the slice: x: 4, y: 4, z: 8 (z_hi: 2, z_lo: 4; z = z_hi * 4 + z_lo), core: 2. Of those that a mesh axis runs over, the one named last changes fastest.
Arguments:
- rhs: float32 [2, 5, 128, 64, 512], P(None, None, 'axial', 'radial', 'pitch'), may hold values from -12 to 12
- jac0: float32 [5, 5, 128, 64, 512], P(None, None, 'axial', 'radial', 'pitch'), may hold values from -1.2 to 9
- shift0: float32 [128, 64, 512], P('axial', 'radial', 'pitch'), may hold values from 0.5 to 3
- jac1: float32 [5, 5, 64, 32, 256], P(None, None, 'axial', 'radial', 'pitch'), may hold values from -1.2 to 9
- shift1: float32 [64, 32, 256], P('axial', 'radial', 'pitch'), may hold values from 0.5 to 3
- jac2: float32 [5, 5, 32, 16, 128], P(None, None, 'axial', 'radial', 'pitch'), may hold values from -1.2 to 9
- shift2: float32 [32, 16, 128], P('axial', 'radial', 'pitch'), may hold values from 0.5 to 3
- blade_mask: int32 [128, 64, 512], P('axial', 'radial', 'pitch'), may hold values 0 or 1
Outputs:
- solution: float32 [2, 5, 128, 64, 512], P(None, None, 'axial', 'radial', 'pitch')
- damping: float32 [], replicated
All inputs are finite; a program needn't handle non-finite values. No bound on the sum of `blade_mask` on one device may be relied on, other than what follows from the above.
Results may differ from a plain program's by a relative error of at most 0.025.
Values sent between devices are 32-bit elements; how exact they have to be, the bound alone decides.
A program may use at most 128 MiB of HBM per device.

v0:
```python
import functools

import jax
import jax.numpy as jnp
from jax import lax
from jax.experimental import pallas as pl
from jax.experimental.pallas import tpu as pltpu
from jax.sharding import PartitionSpec as P

COARSE_SWEEPS = 4
MESH = pl.DeviceIdType.MESH
W = 128
F32 = jnp.float32


class Level:
    def __init__(self, rows, planes, subs, dup):
        self.nr, self.np, self.subs, self.dup = rows, planes, subs, dup
        self.sp = planes * subs
        self.pad = planes + 2
        self.npl = self.pad * subs
        self.nr8 = max(rows, 8)
        self.height = self.nr8 + 16
        self.per = 64 // (dup * self.sp)
        self.packs = -(-10 // self.per)


FINE = Level(16, 8, 1, 1)
MID = Level(8, 4, 2, 2)
COARSE = Level(4, 2, 2, 4)


def lanes(rows):
    return lax.broadcasted_iota(jnp.int32, (rows, W), 1)


def roll(x, shift):
    return pltpu.roll(x, shift, 1)


def join(a, b):
    return jnp.where((lanes(a.shape[0]) & 1) == 0, a, b)


def split(w):
    even = (lanes(w.shape[0]) & 1) == 0
    return jnp.where(even, w, roll(w, 1)), jnp.where(even, roll(w, W - 1), w)


def scratch():
    shapes = {}

    def vmem(name, *shape):
        shapes[name] = pltpu.VMEM(shape, F32)

    for tag, lv in (("0", FINE), ("1", MID), ("2", COARSE)):
        vmem("ua" + tag, 10 * lv.npl, lv.height, W)
        vmem("ub" + tag, 10 * lv.npl, lv.height, W)
        vmem("f" + tag, 10 * lv.sp, lv.nr8, W)
        vmem("c" + tag, 26 * lv.sp, lv.nr8, W)
        vmem("sr" + tag, 5 * lv.sp, lv.nr8, W)
        vmem("si" + tag, 5 * lv.sp, lv.nr8, W)
    for r in range(ROUNDS):
        lv = LEVEL_OF[r]
        tag = "_%d" % r
        fields, ends = (10, 2) if lv is FINE else (5, 4)
        vmem("axs" + tag, ends, fields, lv.nr8, W)
        vmem("axr" + tag, ends, fields, lv.nr8, W)
        vmem("rs" + tag, 2, lv.sp, 16 if lv is FINE else 8, W)
        vmem("rr" + tag, 2, lv.sp, 16 if lv is FINE else 8, W)
        vmem("ps" + tag, lv.packs, lv.nr8, W)
        vmem("pr" + tag, 2, lv.packs, lv.nr8, W)
        vmem("m" + tag, lv.packs, lv.nr8, W)
    vmem("part_s", 2, 5, 8, W)
    vmem("part_r", 2, 5, 8, W)
    vmem("f_part", 40, 8, W)
    vmem("gs", 20, 8, W)
    vmem("gr", 20, 8, W)
    vmem("c1s", 52, 8, W)
    vmem("c1r", 52, 8, W)
    vmem("c2s", 26, 8, W)
    vmem("c2r", 26, 8, W)
    vmem("t", 10, 48, W)
    vmem("j1", 104, 8, 64)
    vmem("j2", 52, 4, 32)
    vmem("j2p", 52, 8, 32)
    vmem("outv", 80, 16, W)
    vmem("red0", 16, 8, W)
    vmem("red1", 16, 8, W)
    shapes["mask"] = pltpu.VMEM((8, 16, W), jnp.int32)
    shapes["ss"] = pltpu.SemaphoreType.DMA((COPIES,))
    shapes["rs"] = pltpu.SemaphoreType.DMA((COPIES,))
    shapes["ls"] = pltpu.SemaphoreType.DMA((10,))
    return shapes


LEVEL_OF = [FINE, FINE, MID, MID, COARSE, COARSE, COARSE, MID, MID, MID, FINE]
ROUNDS = len(LEVEL_OF)
COPIES = 128


def kernel(sizes, names, *refs):
    rhs, jac0, shift0, jac1, shift1, jac2, shift2, blade = refs[:8]
    out, damp = refs[8:10]
    v = dict(zip(names, refs[10:]))
    n_ax, n_rad, n_pit, cells = sizes

    ax, rad, pit = lax.axis_index("axial"), lax.axis_index("radial"), lax.axis_index("pitch")
    core = lax.rem(ax, 2)
    zh = lax.rem(ax // 2, 2)
    x = ax // 4
    nx = n_ax // 4
    z = zh * n_pit + pit
    nz = 2 * n_pit

    def place(xx, yy, zz, cc):
        return {"axial": xx * 4 + (zz // n_pit) * 2 + cc, "radial": yy, "pitch": lax.rem(zz, n_pit)}

    up, down = {"axial": ax + 1}, {"axial": ax - 1}
    has_up, has_down = ax < n_ax - 1, ax > 0
    north, south = {"radial": rad + 1}, {"radial": rad - 1}
    has_north, has_south = rad < n_rad - 1, rad > 0
    east, west = {"pitch": lax.rem(pit + 1, n_pit)}, {"pitch": lax.rem(pit + n_pit - 1, n_pit)}
    z_east, z_west = place(x, rad, lax.rem(z + 1, nz), core), place(x, rad, lax.rem(z + nz - 1, nz), core)
    twin = {"axial": ax + 2 - 4 * zh}
    sibling = {"axial": ax + 1 - 2 * core}
    hop = {"axial": ax + 6 * core - 3}
    has_hop = jnp.logical_or(jnp.logical_and(core == 0, x > 0), jnp.logical_and(core == 1, x < nx - 1))
    wrap_e = pit == n_pit - 1
    wrap_w = pit == 0

    def when(cond, act):
        if cond is None:
            act()
        else:
            pl.when(cond)(act)

    local = [
        (rhs, v["f0"]),
        (jac0, v["c0"].at[pl.ds(0, 200)]),
        (shift0, v["c0"].at[pl.ds(200, 8)]),
        (jac1, v["j1"].at[pl.ds(0, 100)]),
        (shift1, v["j1"].at[pl.ds(100, 4)]),
        (jac2, v["j2"].at[pl.ds(0, 50)]),
        (shift2, v["j2"].at[pl.ds(50, 2)]),
        (blade, v["mask"]),
    ]
    loads = [pltpu.make_async_copy(a, b, v["ls"].at[i]) for i, (a, b) in enumerate(local)]
    for c in loads:
        c.start()

    barrier = pltpu.get_barrier_semaphore()
    greet = [
        (up, has_up),
        (down, has_down),
        (north, has_north),
        (south, has_south),
        (east, None),
        (west, None),
        (twin, None),
        (hop, has_hop),
        (z_east, wrap_e),
        (z_west, wrap_w),
    ]
    for dev, cond in greet:
        when(cond, lambda dev=dev: pl.semaphore_signal(barrier, inc=1, device_id=dev, device_id_type=MESH))

    counter = [0]
    sent = []

    class Msg:
        def __init__(self, src, dst, dev, send_if=None, recv_if=None, landing=None):
            i = counter[0]
            counter[0] += 1
            make = lambda d: pltpu.make_async_remote_copy(
                src_ref=src, dst_ref=d, send_sem=v["ss"].at[i], recv_sem=v["rs"].at[i], device_id=dev, device_id_type=MESH
            )
            self.copy = make(dst)
            self.into = self.copy if landing is None else make(landing)
            self.send_if, self.recv_if = send_if, recv_if

        def start(self):
            when(self.send_if, self.copy.start)
            sent.append(self)

        def recv(self):
            when(self.recv_if, self.into.wait_recv)

    for r in range(ROUNDS):
        tag = "_%d" % r
        axr, rr = v["axr" + tag], v["rr" + tag]

        def zero(ref, i):
            ref[i] = jnp.zeros(ref.shape[1:], F32)

        if LEVEL_OF[r] is FINE:
            when(jnp.logical_not(has_down), functools.partial(zero, axr, 0))
            when(jnp.logical_not(has_up), functools.partial(zero, axr, 1))
        else:
            when(jnp.logical_and(core == 0, x == 0), functools.partial(zero, axr, 0))
            when(jnp.logical_and(core == 1, x == nx - 1), functools.partial(zero, axr, 3))
        when(jnp.logical_not(has_south), functools.partial(zero, rr, 0))
        when(jnp.logical_not(has_north), functools.partial(zero, rr, 1))
    part_s, part_r = v["part_s"], v["part_r"]
    when(jnp.logical_not(has_down), lambda: zero(part_r, 0))
    when(jnp.logical_not(has_up), lambda: zero(part_r, 1))

    def planes(lv, body, lo=0, hi=None, step=1):
        hi = lv.np if hi is None else hi
        for s in range(lv.subs):

            def go(a, carry, s=s):
                a = lo + a * step
                body(s * lv.np + a, s * lv.pad + 1 + a)
                return carry

            lax.fori_loop(0, (hi - lo + step - 1) // step, go, 0)

    def coefficients(lv, tag):
        c, sr, si = v["c" + tag], v["sr" + tag], v["si" + tag]

        def body(sp, carry):
            s = c[25 * lv.sp + sp, 0 : lv.nr, :]
            for i in range(5):
                d = c[6 * i * lv.sp + sp, 0 : lv.nr, :]
                denom = d * d + s * s
                inv = 0.7 / jnp.where(denom > 0, denom, 1.0)
                sr[i * lv.sp + sp, 0 : lv.nr, :] = d * inv
                si[i * lv.sp + sp, 0 : lv.nr, :] = s * inv
            return carry

        lax.fori_loop(0, lv.sp, body, 0)

    def smooth(lv, tag, sp, res):
        sr, si = v["sr" + tag], v["si" + tag]
        new = [None] * 10
        for i in range(5):
            a, b = sr[i * lv.sp + sp, 0 : lv.nr, :], si[i * lv.sp + sp, 0 : lv.nr, :]
            new[i] = a * res[i] + b * res[5 + i]
            new[5 + i] = a * res[5 + i] - b * res[i]
        return new

    def first(lv, tag, u):
        f = v["f" + tag]

        def body(sp, pp):
            new = smooth(lv, tag, sp, [f[k * lv.sp + sp, 0 : lv.nr, :] for k in range(10)])
            for k in range(10):
                u[k * lv.npl + pp, 8 : 8 + lv.nr, :] = new[k]

        planes(lv, body)

    def pack_inplane(lv, u, r):
        tag = "_%d" % r
        rs, ps = v["rs" + tag], v["ps" + tag]
        d, nr = lv.dup, lv.nr
        group = lanes(nr) // (2 * d)
        carry = tuple(jnp.zeros((nr, W), F32) for _ in range(lv.packs))
        for s in range(lv.subs):

            def body(a, carry, s=s):
                sp, pp = s * lv.np + a, s * lv.pad + 1 + a
                packed = list(carry)
                xs = [u[k * lv.npl + pp, 8 : 8 + nr, :] for k in range(10)]
                for k in range(10):
                    slot, j = (k % lv.per) * lv.sp + sp, k // lv.per
                    packed[j] = jnp.where(group == slot, roll(xs[k], d + 2 * d * slot), packed[j])
                faces = xs if lv is FINE else [join(xs[k], xs[5 + k]) for k in range(5)]
                for k, w in enumerate(faces):
                    rs[0, sp, k : k + 1, :] = w[0:1, :]
                    rs[1, sp, k : k + 1, :] = w[nr - 1 : nr, :]
                return tuple(packed)

            carry = lax.fori_loop(0, lv.np, body, carry)
        for j in range(lv.packs):
            ps[j, 0:nr, :] = carry[j]

    def inplane_msgs(lv, r):
        tag = "_%d" % r
        rs, rr, ps, pr = (v[n + tag] for n in ("rs", "rr", "ps", "pr"))
        e, w = (east, west) if lv is FINE else (z_east, z_west)
        return [
            Msg(ps, pr.at[0], e),
            Msg(ps, pr.at[1], w),
            Msg(rs.at[1], rr.at[0], north, has_north, has_south),
            Msg(rs.at[0], rr.at[1], south, has_south, has_north),
        ]

    def pack_axial(lv, u, r):
        axs = v["axs_%d" % r]
        nr = lv.nr
        if lv is FINE:

            def body(k, carry):
                axs[0, k] = u[k * lv.npl + 1, 8 : 8 + nr, :]
                axs[1, k] = u[k * lv.npl + lv.np, 8 : 8 + nr, :]
                return carry

            lax.fori_loop(0, 10, body, 0)
            return
        for q in range(4):
            pp = (q // 2) * lv.pad + (1 if q % 2 == 0 else lv.np)
            for k in range(5):
                axs[q, k, 0:nr, :] = join(
                    u[k * lv.npl + pp, 8 : 8 + nr, :], u[(5 + k) * lv.npl + pp, 8 : 8 + nr, :]
                )

    def axial_msgs(lv, r):
        axs, axr = v["axs_%d" % r], v["axr_%d" % r]
        if lv is FINE:
            return [
                Msg(axs.at[1], axr.at[0], up, has_up, has_down),
                Msg(axs.at[0], axr.at[1], down, has_down, has_up),
            ]
        return [
            Msg(axs.at[3 * core], axr.at[3 - 3 * core], hop, has_hop, has_hop, landing=axr.at[3 * core]),
            Msg(axs.at[pl.ds(1 - core, 3)], axr.at[pl.ds(core, 3)], sibling, landing=axr.at[pl.ds(1 - core, 3)]),
        ]

    def land_axial(lv, u, r):
        axr = v["axr_%d" % r]
        nr = lv.nr
        if lv is FINE:

            def body(k, carry):
                u[k * lv.npl, 8 : 8 + nr, :] = axr[0, k]
                u[k * lv.npl + lv.np + 1, 8 : 8 + nr, :] = axr[1, k]
                return carry

            lax.fori_loop(0, 10, body, 0)
            return
        for q in range(4):
            pp = (q // 2) * lv.pad + (0 if q % 2 == 0 else lv.np + 1)
            for k in range(5):
                re, im = split(axr[q, k, 0:nr, :])
                u[k * lv.npl + pp, 8 : 8 + nr, :] = re
                u[(5 + k) * lv.npl + pp, 8 : 8 + nr, :] = im

    def land_inplane(lv, u, r):
        tag = "_%d" % r
        rr, pr, m = (v[n + tag] for n in ("rr", "pr", "m"))
        d, nr = lv.dup, lv.nr
        low = (lanes(nr) & (2 * d - 1)) < d
        for j in range(lv.packs):
            m[j, 0:nr, :] = jnp.where(low, roll(pr[1, j, 0:nr, :], W - d), roll(pr[0, j, 0:nr, :], d))

        def body(sp, pp):
            for side, row in ((0, 7), (1, 8 + nr)):
                if lv is FINE:
                    for k in range(10):
                        u[k * lv.npl + pp, row : row + 1, :] = rr[side, sp, k : k + 1, :]
                else:
                    re, im = split(rr[side, sp])
                    for k in range(5):
                        u[k * lv.npl + pp, row : row + 1, :] = re[k : k + 1, :]
                        u[(5 + k) * lv.npl + pp, row : row + 1, :] = im[k : k + 1, :]

        planes(lv, body)

    def side_halo(lv, r):
        m = v["m_%d" % r]
        d = lv.dup
        return lambda k, sp: roll(m[k // lv.per, 0 : lv.nr, :], W - d - 2 * d * ((k % lv.per) * lv.sp + sp))

    def residual(lv, tag, u, sp, pp, halo):
        f, c = v["f" + tag], v["c" + tag]
        d, nr = lv.dup, lv.nr
        lane = lanes(nr)
        first_lane, last_lane = lane < d, lane >= W - d
        xs, res = [], []
        for k in range(10):
            b = k * lv.npl + pp
            c0 = u[b, 8 : 8 + nr, :]
            y = f[k * lv.sp + sp, 0:nr, :] + (u[b + 1, 8 : 8 + nr, :] + u[b - 1, 8 : 8 + nr, :])
            y = y + (u[b, 7 : 7 + nr, :] + u[b, 9 : 9 + nr, :])
            h = halo(k, sp)
            y = y + (jnp.where(first_lane, h, roll(c0, d)) + jnp.where(last_lane, h, roll(c0, W - d)))
            xs.append(c0)
            res.append(y)
        s = c[25 * lv.sp + sp, 0:nr, :]
        for i in range(5):
            re, im = res[i] + s * xs[5 + i], res[5 + i] - s * xs[i]
            for j in range(5):
                a = c[(5 * i + j) * lv.sp + sp, 0:nr, :]
                re = re - a * xs[j]
                im = im - a * xs[5 + j]
            res[i], res[5 + i] = re, im
        return xs, res

    def sweep(lv, tag, u, new, halo):
        def body(sp, pp):
            xs, res = residual(lv, tag, u, sp, pp, halo)
            corr = smooth(lv, tag, sp, res)
            for k in range(10):
                new[k * lv.npl + pp, 8 : 8 + lv.nr, :] = xs[k] + corr[k]

        return body

    t = v["t"]

    def fold(lv, k, y):
        d, nr = lv.dup, lv.nr
        y = y + jnp.where((lanes(nr) & d) == 0, roll(y, W - d), roll(y, d))
        t[k, 0:nr, :] = y
        return t[k, pl.ds(0, nr // 2, stride=2), :] + t[k, pl.ds(1, nr // 2, stride=2), :]

    def exchange(lv, u, r):
        pack_axial(lv, u, r)
        a = axial_msgs(lv, r)
        for msg in a:
            msg.start()
        pack_inplane(lv, u, r)
        b = inplane_msgs(lv, r)
        for msg in b:
            msg.start()
        for msg in b:
            msg.recv()
        land_inplane(lv, u, r)
        for msg in a:
            msg.recv()
        land_axial(lv, u, r)

    ua, ub = v["ua0"], v["ub0"]
    f1, c1, c2 = v["f1"], v["c1"], v["c2"]

    for c in loads[:3]:
        c.wait()
    coefficients(FINE, "0")
    first(FINE, "0", ua)

    pack_axial(FINE, ua, 0)
    count = sum(jnp.int32(1) if cond is None else cond.astype(jnp.int32) for _, cond in greet)
    pl.semaphore_wait(barrier, count)
    a0 = axial_msgs(FINE, 0)
    for msg in a0:
        msg.start()
    pack_inplane(FINE, ua, 0)
    b0 = inplane_msgs(FINE, 0)
    for msg in b0:
        msg.start()

    for c in loads[3:]:
        c.wait()

    def spreader(n):
        return (
            lax.broadcasted_iota(jnp.int32, (n, W), 1) // (W // n) == lax.broadcasted_iota(jnp.int32, (n, W), 0)
        ).astype(F32)

    def spread(cells_in, n):
        rows = cells_in.shape[0] * 8
        y = jnp.dot(
            cells_in.reshape(rows, n), spreader(n), precision=lax.Precision.HIGHEST, preferred_element_type=F32
        )
        return y.reshape(cells_in.shape[0], 8, W)

    j1, j2, j2p = v["j1"], v["j2"], v["j2p"]
    c1s, c1r, c2s, c2r = v["c1s"], v["c1r"], v["c2s"], v["c2r"]

    def spread1(e, carry):
        c1[pl.ds(e * 8 + zh * 4, 4)] = spread(j1[pl.ds(e * 4, 4)], 64)
        return carry

    lax.fori_loop(0, 26, spread1, 0)

    def place2(i, carry):
        j2p[i, 0:4, :] = j2[i]
        j2p[i, 4:8, :] = j2[i]
        return carry

    lax.fori_loop(0, 52, place2, 0)

    def spread2(e, carry):
        y = spread(j2p[pl.ds(e * 4, 4)], 32)
        c2[pl.ds(e * 8 + zh * 2, 2)] = y[0:2]
        c2[pl.ds(e * 8 + 4 + zh * 2, 2)] = y[2:4]
        return carry

    lax.fori_loop(0, 13, spread2, 0)

    def join1(e, carry):
        for a in range(4):
            c1s[e * 4 + a] = join(c1[e * 8 + zh * 4 + a], c1[(e + 13) * 8 + zh * 4 + a])
        for a in range(2):
            c2s[e * 2 + a] = join(c2[e * 4 + zh * 2 + a], c2[(e + 13) * 4 + zh * 2 + a])
        return carry

    lax.fori_loop(0, 13, join1, 0)

    def clear(k, carry):
        ub[k * FINE.npl] = jnp.zeros((32, W), F32)
        ub[k * FINE.npl + FINE.np + 1] = jnp.zeros((32, W), F32)
        return carry

    lax.fori_loop(0, 10, clear, 0)

    for msg in b0:
        msg.recv()
    land_inplane(FINE, ua, 0)
    body = sweep(FINE, "0", ua, ub, side_halo(FINE, 0))
    planes(FINE, body, 1, 7)
    for msg in a0:
        msg.recv()
    land_axial(FINE, ua, 0)
    planes(FINE, body, 0, 8, 7)

    for end in range(2):
        for k in range(5):
            pp = 1 if end == 0 else FINE.np
            part_s[end, k] = join(
                fold(FINE, k, ub[k * FINE.npl + pp, 8:24, :]),
                fold(FINE, 5 + k, ub[(5 + k) * FINE.npl + pp, 8:24, :]),
            )
    parts = [
        Msg(part_s.at[1], part_r.at[0], up, has_up, has_down),
        Msg(part_s.at[0], part_r.at[1], down, has_down, has_up),
    ]
    for msg in parts:
        msg.start()
    pack_inplane(FINE, ub, 1)
    b1 = inplane_msgs(FINE, 1)
    for msg in b1:
        msg.start()
    mc1 = Msg(c1s, c1r, twin)
    mc2 = Msg(c2s, c2r, twin)
    mc1.start()
    mc2.start()
    for msg in b1:
        msg.recv()
    land_inplane(FINE, ub, 1)
    f_part = v["f_part"]
    halo1 = side_halo(FINE, 1)

    def restrict0(a, carry):
        _, r0 = residual(FINE, "0", ub, 2 * a, 2 * a + 1, halo1)
        _, r1 = residual(FINE, "0", ub, 2 * a + 1, 2 * a + 2, halo1)
        for k in range(10):
            f_part[k * 4 + a] = 0.125 * fold(FINE, k, r0[k] + r1[k])
        return carry

    lax.fori_loop(0, 4, restrict0, 0)
    for msg in parts:
        msg.recv()
    gs, gr = v["gs"], v["gr"]
    for k in range(5):
        for end, a in ((0, 0), (1, 3)):
            re, im = split(part_r[end, k])
            f_part[k * 4 + a] = f_part[k * 4 + a] + 0.125 * re
            f_part[(5 + k) * 4 + a] = f_part[(5 + k) * 4 + a] + 0.125 * im

    def gather(i, carry):
        gs[i] = join(f_part[i], f_part[20 + i])
        return carry

    lax.fori_loop(0, 20, gather, 0)
    mg = Msg(gs, gr, twin)
    mg.start()
    pack_axial(FINE, ub, 1)
    a1 = axial_msgs(FINE, 1)
    for msg in a1:
        msg.start()
    for k in range(10):
        f1[pl.ds(k * 8 + zh * 4, 4)] = f_part[k * 4 : k * 4 + 4]
    mc1.recv()
    mc2.recv()

    def split1(e, carry):
        for a in range(4):
            lo, hi = split(c1r[e * 4 + a])
            c1[e * 8 + (1 - zh) * 4 + a] = lo
            c1[(e + 13) * 8 + (1 - zh) * 4 + a] = hi
        for a in range(2):
            lo, hi = split(c2r[e * 2 + a])
            c2[e * 4 + (1 - zh) * 2 + a] = lo
            c2[(e + 13) * 4 + (1 - zh) * 2 + a] = hi
        return carry

    lax.fori_loop(0, 13, split1, 0)
    coefficients(MID, "1")
    coefficients(COARSE, "2")
    mg.recv()

    def land_gather(i, carry):
        re, im = split(gr[i])
        k, a = i // 4, lax.rem(i, 4)
        f1[k * 8 + (1 - zh) * 4 + a] = re
        f1[(k + 5) * 8 + (1 - zh) * 4 + a] = im
        return carry

    lax.fori_loop(0, 20, land_gather, 0)

    m_a, m_b = v["ua1"], v["ub1"]
    first(MID, "1", m_a)
    exchange(MID, m_a, 2)
    planes(MID, sweep(MID, "1", m_a, m_b, side_halo(MID, 2)))
    exchange(MID, m_b, 3)
    halo3 = side_halo(MID, 3)
    f2 = v["f2"]
    for s in range(2):

        def restrict1(a, carry, s=s):
            _, r0 = residual(MID, "1", m_b, s * 4 + 2 * a, s * 6 + 2 * a + 1, halo3)
            _, r1 = residual(MID, "1", m_b, s * 4 + 2 * a + 1, s * 6 + 2 * a + 2, halo3)
            for k in range(10):
                f2[k * 4 + s * 2 + a, 0:4, :] = 0.125 * fold(MID, k, r0[k] + r1[k])
            return carry

        lax.fori_loop(0, 2, restrict1, 0)

    q_a, q_b = v["ua2"], v["ub2"]
    first(COARSE, "2", q_a)
    for step in range(COARSE_SWEEPS - 1):
        exchange(COARSE, q_a, 4 + step)
        planes(COARSE, sweep(COARSE, "2", q_a, q_b, side_halo(COARSE, 4 + step)))
        q_a, q_b = q_b, q_a

    for s in range(2):

        def prolong1(a, carry, s=s):
            for k in range(10):
                w = q_a[k * COARSE.npl + s * 4 + 1 + a // 2, 8:16, :]
                t[k, pl.ds(0, 8, stride=2), :] = w
                t[k, pl.ds(1, 8, stride=2), :] = w
                b = k * MID.npl + s * 6 + 1 + a
                m_b[b, 8:16, :] = m_b[b, 8:16, :] + t[k, 0:8, :]
            return carry

        lax.fori_loop(0, 4, prolong1, 0)
    exchange(MID, m_b, 7)
    planes(MID, sweep(MID, "1", m_b, m_a, side_halo(MID, 7)))
    exchange(MID, m_a, 8)
    planes(MID, sweep(MID, "1", m_a, m_b, side_halo(MID, 8)))

    for msg in a1:
        msg.recv()
    land_axial(FINE, ub, 1)
    exchange(MID, m_b, 9)

    def prolong0(q, carry):
        for k in range(10):
            w = m_b[k * MID.npl + zh * 6 + (q + 1) // 2]
            t[k, pl.ds(0, 24, stride=2), :] = w
            t[k, pl.ds(1, 24, stride=2), :] = w
            ub[k * FINE.npl + q] = ub[k * FINE.npl + q] + t[k, 8:40, :]
        return carry

    lax.fori_loop(0, 10, prolong0, 0)
    halo9 = side_halo(MID, 9)

    def halo_up(k, sp):
        w = halo9(k, zh * 4 + sp // 2)
        t[k, pl.ds(0, 8, stride=2), :] = w
        t[k, pl.ds(1, 8, stride=2), :] = w
        return halo1(k, sp) + t[k, 0:16, :]

    planes(FINE, sweep(FINE, "0", ub, ua, halo_up))

    pack_axial(FINE, ua, 10)
    a10 = axial_msgs(FINE, 10)
    for msg in a10:
        msg.start()
    pack_inplane(FINE, ua, 10)
    b10 = inplane_msgs(FINE, 10)
    for msg in b10:
        msg.start()
    for msg in b10:
        msg.recv()
    land_inplane(FINE, ua, 10)
    outv, mask = v["outv"], v["mask"]
    halo10 = side_halo(FINE, 10)

    def last(a, acc):
        xs, res = residual(FINE, "0", ua, a, a + 1, halo10)
        corr = smooth(FINE, "0", a, res)
        new = [xs[k] + corr[k] for k in range(10)]
        for k in range(10):
            outv[k * 8 + a] = new[k]
        return acc + mask[a].astype(F32) * (new[4] * new[6] - new[9] * new[1])

    acc = lax.fori_loop(1, 7, last, jnp.zeros((16, W), F32))
    for msg in a10:
        msg.recv()
    land_axial(FINE, ua, 10)
    acc = lax.fori_loop(0, 2, lambda i, c: last(7 * i, c), acc)
    store = pltpu.make_async_copy(outv, out, v["ls"].at[8])
    store.start()

    red0, red1 = v["red0"], v["red1"]
    mine0 = x * n_rad + rad
    red0[mine0] = acc[0:8] + acc[8:16]
    msgs = []
    n0 = nx * n_rad
    for off in range(1, n0):
        to = lax.rem(mine0 + off, n0)
        back = lax.rem(mine0 + n0 - off, n0)
        msgs.append(
            Msg(red0.at[mine0], red0.at[mine0], place(to // n_rad, lax.rem(to, n_rad), z, core), landing=red0.at[back])
        )
    for msg in msgs:
        msg.start()
    for msg in msgs:
        msg.recv()
    total = red0[0]
    for i in range(1, n0):
        total = total + red0[i]
    mine1 = z * 2 + core
    red1[mine1] = total
    msgs = []
    n1 = nz * 2
    for off in range(1, n1):
        to = lax.rem(mine1 + off, n1)
        back = lax.rem(mine1 + n1 - off, n1)
        msgs.append(Msg(red1.at[mine1], red1.at[mine1], place(x, rad, to // 2, lax.rem(to, 2)), landing=red1.at[back]))
    for msg in msgs:
        msg.start()
    for msg in msgs:
        msg.recv()
    total = red1[0]
    for i in range(1, n1):
        total = total + red1[i]
    damp[0, 0] = jnp.sum(total) * (25.0 / jnp.sqrt(jnp.float32(cells)))
    store.wait()
    for msg in sent:
        when(msg.send_if, msg.copy.wait_send)


def solution(mesh):
    sizes = (mesh.shape["axial"], mesh.shape["radial"], mesh.shape["pitch"])

    def on_device(rhs, jac0, shift0, jac1, shift1, jac2, shift2, blade_mask):
        cells = shift0.size * sizes[0] * sizes[1] * sizes[2]
        shapes = scratch()
        out, damp = pl.pallas_call(
            functools.partial(kernel, sizes + (cells,), tuple(shapes)),
            out_shape=(jax.ShapeDtypeStruct((80, 16, W), F32), jax.ShapeDtypeStruct((1, 1), F32)),
            in_specs=[pl.BlockSpec(memory_space=pl.ANY)] * 8,
            out_specs=(pl.BlockSpec(memory_space=pl.ANY), pl.BlockSpec(memory_space=pltpu.SMEM)),
            scratch_shapes=list(shapes.values()),
            compiler_params=pltpu.CompilerParams(
                collective_id=0, has_side_effects=True, vmem_limit_bytes=48 * 1024 * 1024
            ),
        )(
            rhs.reshape(80, 16, W),
            jac0.reshape(200, 16, W),
            shift0,
            jac1.reshape(100, 8, 64),
            shift1,
            jac2.reshape(50, 4, 32),
            shift2,
            blade_mask,
        )
        return out.reshape(rhs.shape), damp.reshape(())

    spec = P(None, None, "axial", "radial", "pitch")
    flat = P("axial", "radial", "pitch")
    return jax.shard_map(
        on_device,
        mesh=mesh,
        in_specs=(spec, spec, flat, spec, flat, spec, flat, flat),
        out_specs=(spec, P()),
        check_vma=False,
    )
```

profile of v0, /device:TPU:1, one launch (start us, length us, event | category | flops | bytes accessed | tf_op | source)
XLA Modules:
  0.0 120.7 jit_solution(1508177575115899592)
XLA Ops:
  0.6 0.0 copy-start
  0.6 1.4 %copy-done = f32[5,5,8,16,128]{4,3,2,1,0:T(8,128)S(1)} copy-done((f32[5,5,8,16,128]{4,3,2,1,0:T(8,128)S(1)}, f32[5,5,8,16,128]{4,3,2,1,0:T(8,128)}, u32[]{:S(2)}) %copy-start) | copy-done | bytes 1638424
  2.1 0.0 copy-start.1
  2.1 1.1 copy-done.1
  3.2 0.0 copy-start.2
  3.2 1.0 copy-done.2
  4.2 0.0 copy-start.3
  4.2 0.9 copy-done.3
  5.0 0.0 copy-start.4
  5.1 0.8 copy-done.4
  5.9 0.0 copy-start.5
  5.9 0.8 copy-done.5
  6.7 0.0 copy-start.6
  6.7 0.7 copy-done.6
  7.4 0.0 copy-start.7
  7.4 0.7 copy-done.7
  8.1 109.9 %shard_map.95 = (f32[80,16,128]{2,1,0:T(8,128)S(1)}, f32[1,1]{1,0:T(1,128)}) custom-call(f32[80,16,128]{2,1,0:T(8,128)S(1)} %bitcast.8, f32[200,16,128]{2,1,0:T(8,128)S(1)} %bitcast.6, f32[8,16,128]{2,1,0:T(8,128)S(1)} %copy-done.4, f32[100,8,64]{2,1,0:T(8,128)S(1)} %bitcast.9, f32[4,8,64]{2,1,0:T(8,128)S(1)} %copy-done.6, f32[50,4,32]{2,1,0:T(4,128)S(1)} %bitcast.10, ...), custom_call_target="tpu_custom_call" | custom-call | tf_op jit(solution)/shard_map/pallas_call | solution.py:733
  118.1 0.8 copy.12
Async XLA Ops:
  0.6 1.4 %copy-start = (f32[5,5,8,16,128]{4,3,2,1,0:T(8,128)S(1)}, f32[5,5,8,16,128]{4,3,2,1,0:T(8,128)}, u32[]{:S(2)}) copy-start(f32[5,5,8,16,128]{4,3,2,1,0:T(8,128)} %param.9) | copy-start | bytes 4915204
  2.1 1.1 copy-start.1
  3.2 1.0 copy-start.2
  4.2 0.9 copy-start.3
  5.0 0.8 copy-start.4
  5.9 0.8 copy-start.5
  6.7 0.7 copy-start.6
  7.4 0.7 copy-start.7
where the time goes:
time: 121 us
  Pallas kernels  110 us (91%)
  local copies, waits for them, and re-layouts  8.33 us (7%)
  between operations  2.47 us (2%)
    pallas_call x1, Pallas kernels, on_device(): pl.pallas_call(functools.partial(kernel, sizes + (cells,), tuple(shapes))...  110 us
    unnamed x17, local copies, waits for them, and re-layouts  8.33 us

commit v1 on v0

--- a/solution.py
+++ b/solution.py
@@ -78,13 +78,12 @@
     vmem("gr", 20, 8, W)
     vmem("c1s", 52, 8, W)
     vmem("c1r", 52, 8, W)
-    vmem("c2s", 26, 8, W)
-    vmem("c2r", 26, 8, W)
+    vmem("c2s", 13, 8, W)
+    vmem("c2r", 13, 8, W)
     vmem("t", 10, 48, W)
     vmem("j1", 104, 8, 64)
     vmem("j2", 52, 4, 32)
-    vmem("j2p", 52, 8, 32)
-    vmem("outv", 80, 16, W)
+    vmem("j2p", 26, 8, 32)
     vmem("red0", 16, 8, W)
     vmem("red1", 16, 8, W)
     shapes["mask"] = pltpu.VMEM((8, 16, W), jnp.int32)
@@ -97,6 +96,7 @@
 LEVEL_OF = [FINE, FINE, MID, MID, COARSE, COARSE, COARSE, MID, MID, MID, FINE]
 ROUNDS = len(LEVEL_OF)
 COPIES = 128
+UNROLL = 2
 
 
 def kernel(sizes, names, *refs):
@@ -241,39 +241,53 @@
         return new
 
     def first(lv, tag, u):
+        step = first_plane(lv, tag, u)
+        planes(lv, lambda sp, pp: step(sp, pp) and None)
+
+    def first_plane(lv, tag, u):
         f = v["f" + tag]
 
-        def body(sp, pp):
+        def step(sp, pp):
             new = smooth(lv, tag, sp, [f[k * lv.sp + sp, 0 : lv.nr, :] for k in range(10)])
             for k in range(10):
                 u[k * lv.npl + pp, 8 : 8 + lv.nr, :] = new[k]
-
-        planes(lv, body)
-
-    def pack_inplane(lv, u, r):
-        tag = "_%d" % r
-        rs, ps = v["rs" + tag], v["ps" + tag]
+            return new
+
+        return step
+
+    def packing(lv):
+        return tuple(jnp.zeros((lv.nr, W), F32) for _ in range(lv.packs))
+
+    def pack_plane(lv, xs, sp, r, carry):
+        rs = v["rs_%d" % r]
         d, nr = lv.dup, lv.nr
         group = lanes(nr) // (2 * d)
-        carry = tuple(jnp.zeros((nr, W), F32) for _ in range(lv.packs))
+        packed = list(carry)
+        for k in range(10):
+            slot, j = (k % lv.per) * lv.sp + sp, k // lv.per
+            packed[j] = jnp.where(group == slot, roll(xs[k], d + 2 * d * slot), packed[j])
+        faces = xs if lv is FINE else [join(xs[k], xs[5 + k]) for k in range(5)]
+        for k, w in enumerate(faces):
+            rs[0, sp, k : k + 1, :] = w[0:1, :]
+            rs[1, sp, k : k + 1, :] = w[nr - 1 : nr, :]
+        return tuple(packed)
+
+    def pack_inplane(lv, u, r, step=None):
+        ps = v["ps_%d" % r]
+        carry = packing(lv)
         for s in range(lv.subs):
 
             def body(a, carry, s=s):
                 sp, pp = s * lv.np + a, s * lv.pad + 1 + a
-                packed = list(carry)
-                xs = [u[k * lv.npl + pp, 8 : 8 + nr, :] for k in range(10)]
-                for k in range(10):
-                    slot, j = (k % lv.per) * lv.sp + sp, k // lv.per
-                    packed[j] = jnp.where(group == slot, roll(xs[k], d + 2 * d * slot), packed[j])
-                faces = xs if lv is FINE else [join(xs[k], xs[5 + k]) for k in range(5)]
-                for k, w in enumerate(faces):
-                    rs[0, sp, k : k + 1, :] = w[0:1, :]
-                    rs[1, sp, k : k + 1, :] = w[nr - 1 : nr, :]
-                return tuple(packed)
-
-            carry = lax.fori_loop(0, lv.np, body, carry)
+                if step is None:
+                    xs = [u[k * lv.npl + pp, 8 : 8 + lv.nr, :] for k in range(10)]
+                else:
+                    xs = step(sp, pp)
+                return pack_plane(lv, xs, sp, r, carry)
+
+            carry = lax.fori_loop(0, lv.np, body, carry, unroll=UNROLL if lv is not FINE else 2)
         for j in range(lv.packs):
-            ps[j, 0:nr, :] = carry[j]
+            ps[j, 0 : lv.nr, :] = carry[j]
 
     def inplane_msgs(lv, r):
         tag = "_%d" % r
@@ -317,64 +331,69 @@
             Msg(axs.at[pl.ds(1 - core, 3)], axr.at[pl.ds(core, 3)], sibling, landing=axr.at[pl.ds(1 - core, 3)]),
         ]
 
-    def land_axial(lv, u, r):
-        axr = v["axr_%d" % r]
-        nr = lv.nr
-        if lv is FINE:
-
-            def body(k, carry):
-                u[k * lv.npl, 8 : 8 + nr, :] = axr[0, k]
-                u[k * lv.npl + lv.np + 1, 8 : 8 + nr, :] = axr[1, k]
-                return carry
-
-            lax.fori_loop(0, 10, body, 0)
-            return
-        for q in range(4):
-            pp = (q // 2) * lv.pad + (0 if q % 2 == 0 else lv.np + 1)
-            for k in range(5):
-                re, im = split(axr[q, k, 0:nr, :])
-                u[k * lv.npl + pp, 8 : 8 + nr, :] = re
-                u[(5 + k) * lv.npl + pp, 8 : 8 + nr, :] = im
-
-    def land_inplane(lv, u, r):
-        tag = "_%d" % r
-        rr, pr, m = (v[n + tag] for n in ("rr", "pr", "m"))
+    def turn(lv, r):
+        pr, m = v["pr_%d" % r], v["m_%d" % r]
         d, nr = lv.dup, lv.nr
         low = (lanes(nr) & (2 * d - 1)) < d
         for j in range(lv.packs):
             m[j, 0:nr, :] = jnp.where(low, roll(pr[1, j, 0:nr, :], W - d), roll(pr[0, j, 0:nr, :], d))
 
-        def body(sp, pp):
-            for side, row in ((0, 7), (1, 8 + nr)):
-                if lv is FINE:
-                    for k in range(10):
-                        u[k * lv.npl + pp, row : row + 1, :] = rr[side, sp, k : k + 1, :]
-                else:
-                    re, im = split(rr[side, sp])
-                    for k in range(5):
-                        u[k * lv.npl + pp, row : row + 1, :] = re[k : k + 1, :]
-                        u[(5 + k) * lv.npl + pp, row : row + 1, :] = im[k : k + 1, :]
-
-        planes(lv, body)
-
     def side_halo(lv, r):
         m = v["m_%d" % r]
         d = lv.dup
         return lambda k, sp: roll(m[k // lv.per, 0 : lv.nr, :], W - d - 2 * d * ((k % lv.per) * lv.sp + sp))
 
-    def residual(lv, tag, u, sp, pp, halo):
+    def row_halo(lv, r, sp):
+        rr = v["rr_%d" % r]
+        if lv is FINE:
+            return [(rr[0, sp, k : k + 1, :], rr[1, sp, k : k + 1, :]) for k in range(10)]
+        lo, hi = split(rr[0, sp]), split(rr[1, sp])
+        return [(lo[k // 5][k % 5 : k % 5 + 1, :], hi[k // 5][k % 5 : k % 5 + 1, :]) for k in range(10)]
+
+    def ring(nr, d, side, lo, hi):
+        lane, row = lanes(nr), lax.broadcasted_iota(jnp.int32, (nr, W), 0)
+        h = jnp.where((lane < d) | (lane >= W - d), side, 0.0)
+        lo, hi = jnp.broadcast_to(lo, (nr, W)), jnp.broadcast_to(hi, (nr, W))
+        return h + jnp.where(row == 0, lo, jnp.where(row == nr - 1, hi, 0.0))
+
+    def inplane(lv, r, sp):
+        side = side_halo(lv, r)
+        rows = row_halo(lv, r, sp)
+        return [ring(lv.nr, lv.dup, side(k, sp), *rows[k]) for k in range(10)]
+
+    def beside(lv, r, q):
+        axr = v["axr_%d" % r]
+        if lv is FINE:
+            return [axr[q, k] for k in range(10)]
+        both = [split(axr[q, k, 0 : lv.nr, :]) for k in range(5)]
+        return [w[0] for w in both] + [w[1] for w in both]
+
+    def add(lv, tag, u, sp, pp, h):
+        corr = smooth(lv, tag, sp, h)
+        new = []
+        for k in range(10):
+            b = k * lv.npl + pp
+            new.append(u[b, 8 : 8 + lv.nr, :] + corr[k])
+            u[b, 8 : 8 + lv.nr, :] = new[k]
+        return new
+
+    def add_axial(lv, tag, u, r):
+        for q in range(2 * lv.subs):
+            a = 0 if q % 2 == 0 else lv.np - 1
+            s = q // 2
+            add(lv, tag, u, s * lv.np + a, s * lv.pad + 1 + a, beside(lv, r, q))
+
+    def residual(lv, tag, u, sp, pp):
         f, c = v["f" + tag], v["c" + tag]
         d, nr = lv.dup, lv.nr
         lane = lanes(nr)
-        first_lane, last_lane = lane < d, lane >= W - d
         xs, res = [], []
         for k in range(10):
             b = k * lv.npl + pp
             c0 = u[b, 8 : 8 + nr, :]
             y = f[k * lv.sp + sp, 0:nr, :] + (u[b + 1, 8 : 8 + nr, :] + u[b - 1, 8 : 8 + nr, :])
             y = y + (u[b, 7 : 7 + nr, :] + u[b, 9 : 9 + nr, :])
-            h = halo(k, sp)
-            y = y + (jnp.where(first_lane, h, roll(c0, d)) + jnp.where(last_lane, h, roll(c0, W - d)))
+            y = y + (jnp.where(lane < d, 0.0, roll(c0, d)) + jnp.where(lane >= W - d, 0.0, roll(c0, W - d)))
             xs.append(c0)
             res.append(y)
         s = c[25 * lv.sp + sp, 0:nr, :]
@@ -387,14 +406,14 @@
             res[i], res[5 + i] = re, im
         return xs, res
 
-    def sweep(lv, tag, u, new, halo):
+    def interior(lv, tag, u, new):
         def body(sp, pp):
-            xs, res = residual(lv, tag, u, sp, pp, halo)
+            xs, res = residual(lv, tag, u, sp, pp)
             corr = smooth(lv, tag, sp, res)
             for k in range(10):
                 new[k * lv.npl + pp, 8 : 8 + lv.nr, :] = xs[k] + corr[k]
 
-        return body
+        planes(lv, body)
 
     t = v["t"]
 
@@ -404,24 +423,45 @@
         t[k, 0:nr, :] = y
         return t[k, pl.ds(0, nr // 2, stride=2), :] + t[k, pl.ds(1, nr // 2, stride=2), :]
 
-    def exchange(lv, u, r):
+    def send(lv, u, r, step=None):
+        pack_inplane(lv, u, r, step)
+        b = inplane_msgs(lv, r)
+        for msg in b:
+            msg.start()
         pack_axial(lv, u, r)
         a = axial_msgs(lv, r)
         for msg in a:
             msg.start()
-        pack_inplane(lv, u, r)
-        b = inplane_msgs(lv, r)
-        for msg in b:
-            msg.start()
-        for msg in b:
+        return a, b
+
+    def recv(msgs):
+        for msg in msgs:
             msg.recv()
-        land_inplane(lv, u, r)
-        for msg in a:
-            msg.recv()
-        land_axial(lv, u, r)
-
+
+    def finish(lv, tag, u, r, after=None):
+        a, b = flying.pop(r)
+        recv(a)
+        add_axial(lv, tag, u, r)
+        recv(b)
+        turn(lv, r)
+        step = lambda sp, pp: add(lv, tag, u, sp, pp, inplane(lv, r, sp))
+        if after is None:
+            planes(lv, lambda sp, pp: step(sp, pp) and None)
+        else:
+            flying[after] = send(lv, u, after, step)
+
+    flying = {}
     ua, ub = v["ua0"], v["ub0"]
     f1, c1, c2 = v["f1"], v["c1"], v["c2"]
+
+    for tag, lv in (("0", FINE), ("1", MID), ("2", COARSE)):
+        for u in (v["ua" + tag], v["ub" + tag]):
+
+            def clear(i, carry, u=u, lv=lv):
+                u[i] = jnp.zeros((lv.height, W), F32)
+                return carry
+
+            lax.fori_loop(0, 10 * lv.npl, clear, 0)
 
     for c in loads[:3]:
         c.wait()
@@ -439,70 +479,55 @@
     for msg in b0:
         msg.start()
 
+    interior(FINE, "0", ua, ub)
     for c in loads[3:]:
         c.wait()
 
-    def spreader(n):
-        return (
+    def spread(cells_in):
+        count, _, n = cells_in.shape
+        pick = (
             lax.broadcasted_iota(jnp.int32, (n, W), 1) // (W // n) == lax.broadcasted_iota(jnp.int32, (n, W), 0)
         ).astype(F32)
-
-    def spread(cells_in, n):
-        rows = cells_in.shape[0] * 8
         y = jnp.dot(
-            cells_in.reshape(rows, n), spreader(n), precision=lax.Precision.HIGHEST, preferred_element_type=F32
+            cells_in.reshape(count * 8, n), pick, precision=lax.Precision.HIGHEST, preferred_element_type=F32
         )
-        return y.reshape(cells_in.shape[0], 8, W)
+        return y.reshape(count, 8, W)
 
     j1, j2, j2p = v["j1"], v["j2"], v["j2p"]
     c1s, c1r, c2s, c2r = v["c1s"], v["c1r"], v["c2s"], v["c2r"]
 
     def spread1(e, carry):
-        c1[pl.ds(e * 8 + zh * 4, 4)] = spread(j1[pl.ds(e * 4, 4)], 64)
+        y0, y1 = spread(j1[pl.ds(e * 4, 4)]), spread(j1[pl.ds((e + 13) * 4, 4)])
+        c1[pl.ds(e * 8 + zh * 4, 4)] = y0
+        c1[pl.ds((e + 13) * 8 + zh * 4, 4)] = y1
+        for a in range(4):
+            c1s[e * 4 + a] = join(y0[a], y1[a])
         return carry
 
-    lax.fori_loop(0, 26, spread1, 0)
-
-    def place2(i, carry):
-        j2p[i, 0:4, :] = j2[i]
-        j2p[i, 4:8, :] = j2[i]
+    lax.fori_loop(0, 13, spread1, 0, unroll=13)
+
+    def place2(e, carry):
+        j2p[e, 0:4, :] = j2[2 * e]
+        j2p[e, 4:8, :] = j2[2 * e + 1]
         return carry
 
-    lax.fori_loop(0, 52, place2, 0)
-
-    def spread2(e, carry):
-        y = spread(j2p[pl.ds(e * 4, 4)], 32)
-        c2[pl.ds(e * 8 + zh * 2, 2)] = y[0:2]
-        c2[pl.ds(e * 8 + 4 + zh * 2, 2)] = y[2:4]
-        return carry
-
-    lax.fori_loop(0, 13, spread2, 0)
-
-    def join1(e, carry):
-        for a in range(4):
-            c1s[e * 4 + a] = join(c1[e * 8 + zh * 4 + a], c1[(e + 13) * 8 + zh * 4 + a])
-        for a in range(2):
-            c2s[e * 2 + a] = join(c2[e * 4 + zh * 2 + a], c2[(e + 13) * 4 + zh * 2 + a])
-        return carry
-
-    lax.fori_loop(0, 13, join1, 0)
-
-    def clear(k, carry):
-        ub[k * FINE.npl] = jnp.zeros((32, W), F32)
-        ub[k * FINE.npl + FINE.np + 1] = jnp.zeros((32, W), F32)
-        return carry
-
-    lax.fori_loop(0, 10, clear, 0)
-
-    for msg in b0:
-        msg.recv()
-    land_inplane(FINE, ua, 0)
-    body = sweep(FINE, "0", ua, ub, side_halo(FINE, 0))
-    planes(FINE, body, 1, 7)
-    for msg in a0:
-        msg.recv()
-    land_axial(FINE, ua, 0)
-    planes(FINE, body, 0, 8, 7)
+    lax.fori_loop(0, 26, place2, 0, unroll=2)
+    y2 = spread(j2p[...])
+    for e in range(26):
+        c2[e * 4 + zh * 2, 0:4, :] = y2[e, 0:4]
+        c2[e * 4 + zh * 2 + 1, 0:4, :] = y2[e, 4:8]
+    for e in range(13):
+        c2s[e] = join(y2[e], y2[e + 13])
+
+    recv(b0)
+    mc1 = Msg(c1s, c1r, twin)
+    mc2 = Msg(c2s, c2r, twin)
+    mc1.start()
+    mc2.start()
+    turn(FINE, 0)
+    planes(FINE, lambda sp, pp: add(FINE, "0", ub, sp, pp, inplane(FINE, 0, sp)) and None)
+    recv(a0)
+    add_axial(FINE, "0", ub, 0)
 
     for end in range(2):
         for k in range(5):
@@ -521,38 +546,35 @@
     b1 = inplane_msgs(FINE, 1)
     for msg in b1:
         msg.start()
-    mc1 = Msg(c1s, c1r, twin)
-    mc2 = Msg(c2s, c2r, twin)
-    mc1.start()
-    mc2.start()
-    for msg in b1:
-        msg.recv()
-    land_inplane(FINE, ub, 1)
     f_part = v["f_part"]
-    halo1 = side_halo(FINE, 1)
 
     def restrict0(a, carry):
-        _, r0 = residual(FINE, "0", ub, 2 * a, 2 * a + 1, halo1)
-        _, r1 = residual(FINE, "0", ub, 2 * a + 1, 2 * a + 2, halo1)
+        _, r0 = residual(FINE, "0", ub, 2 * a, 2 * a + 1)
+        _, r1 = residual(FINE, "0", ub, 2 * a + 1, 2 * a + 2)
         for k in range(10):
             f_part[k * 4 + a] = 0.125 * fold(FINE, k, r0[k] + r1[k])
         return carry
 
     lax.fori_loop(0, 4, restrict0, 0)
-    for msg in parts:
-        msg.recv()
+    recv(b1)
+    turn(FINE, 1)
+
+    def restrict_halo0(a, carry):
+        h0, h1 = inplane(FINE, 1, 2 * a), inplane(FINE, 1, 2 * a + 1)
+        for k in range(10):
+            f_part[k * 4 + a] = f_part[k * 4 + a] + 0.125 * fold(FINE, k, h0[k] + h1[k])
+        return carry
+
+    lax.fori_loop(0, 4, restrict_halo0, 0)
+    recv(parts)
     gs, gr = v["gs"], v["gr"]
     for k in range(5):
         for end, a in ((0, 0), (1, 3)):
             re, im = split(part_r[end, k])
             f_part[k * 4 + a] = f_part[k * 4 + a] + 0.125 * re
             f_part[(5 + k) * 4 + a] = f_part[(5 + k) * 4 + a] + 0.125 * im
-
-    def gather(i, carry):
+    for i in range(20):
         gs[i] = join(f_part[i], f_part[20 + i])
-        return carry
-
-    lax.fori_loop(0, 20, gather, 0)
     mg = Msg(gs, gr, twin)
     mg.start()
     pack_axial(FINE, ub, 1)
@@ -569,121 +591,136 @@
             lo, hi = split(c1r[e * 4 + a])
             c1[e * 8 + (1 - zh) * 4 + a] = lo
             c1[(e + 13) * 8 + (1 - zh) * 4 + a] = hi
+        lo, hi = split(c2r[e])
         for a in range(2):
-            lo, hi = split(c2r[e * 2 + a])
-            c2[e * 4 + (1 - zh) * 2 + a] = lo
-            c2[(e + 13) * 4 + (1 - zh) * 2 + a] = hi
+            c2[e * 4 + (1 - zh) * 2 + a, 0:4, :] = lo[4 * a : 4 * a + 4]
+            c2[(e + 13) * 4 + (1 - zh) * 2 + a, 0:4, :] = hi[4 * a : 4 * a + 4]
         return carry
 
     lax.fori_loop(0, 13, split1, 0)
     coefficients(MID, "1")
     coefficients(COARSE, "2")
     mg.recv()
-
-    def land_gather(i, carry):
+    for i in range(20):
         re, im = split(gr[i])
-        k, a = i // 4, lax.rem(i, 4)
+        k, a = i // 4, i % 4
         f1[k * 8 + (1 - zh) * 4 + a] = re
         f1[(k + 5) * 8 + (1 - zh) * 4 + a] = im
-        return carry
-
-    lax.fori_loop(0, 20, land_gather, 0)
 
     m_a, m_b = v["ua1"], v["ub1"]
-    first(MID, "1", m_a)
-    exchange(MID, m_a, 2)
-    planes(MID, sweep(MID, "1", m_a, m_b, side_halo(MID, 2)))
-    exchange(MID, m_b, 3)
-    halo3 = side_halo(MID, 3)
+    flying[2] = send(MID, m_a, 2, first_plane(MID, "1", m_a))
+    interior(MID, "1", m_a, m_b)
+    finish(MID, "1", m_b, 2, 3)
     f2 = v["f2"]
     for s in range(2):
 
         def restrict1(a, carry, s=s):
-            _, r0 = residual(MID, "1", m_b, s * 4 + 2 * a, s * 6 + 2 * a + 1, halo3)
-            _, r1 = residual(MID, "1", m_b, s * 4 + 2 * a + 1, s * 6 + 2 * a + 2, halo3)
+            _, r0 = residual(MID, "1", m_b, s * 4 + 2 * a, s * 6 + 2 * a + 1)
+            _, r1 = residual(MID, "1", m_b, s * 4 + 2 * a + 1, s * 6 + 2 * a + 2)
             for k in range(10):
                 f2[k * 4 + s * 2 + a, 0:4, :] = 0.125 * fold(MID, k, r0[k] + r1[k])
             return carry
 
         lax.fori_loop(0, 2, restrict1, 0)
+    a3, b3 = flying.pop(3)
+    recv(a3)
+    recv(b3)
+    turn(MID, 3)
+    for s in range(2):
+        for a in range(2):
+            sp = s * 4 + 2 * a
+            h0, h1, h2 = inplane(MID, 3, sp), inplane(MID, 3, sp + 1), beside(MID, 3, 2 * s + a)
+            for k in range(10):
+                i = k * 4 + s * 2 + a
+                f2[i, 0:4, :] = f2[i, 0:4, :] + 0.125 * fold(MID, k, h0[k] + h1[k] + h2[k])
 
     q_a, q_b = v["ua2"], v["ub2"]
-    first(COARSE, "2", q_a)
-    for step in range(COARSE_SWEEPS - 1):
-        exchange(COARSE, q_a, 4 + step)
-        planes(COARSE, sweep(COARSE, "2", q_a, q_b, side_halo(COARSE, 4 + step)))
+    flying[4] = send(COARSE, q_a, 4, first_plane(COARSE, "2", q_a))
+    for r in range(4, 3 + COARSE_SWEEPS):
+        interior(COARSE, "2", q_a, q_b)
+        finish(COARSE, "2", q_b, r, r + 1 if r < 2 + COARSE_SWEEPS else None)
         q_a, q_b = q_b, q_a
 
-    for s in range(2):
-
-        def prolong1(a, carry, s=s):
-            for k in range(10):
-                w = q_a[k * COARSE.npl + s * 4 + 1 + a // 2, 8:16, :]
-                t[k, pl.ds(0, 8, stride=2), :] = w
-                t[k, pl.ds(1, 8, stride=2), :] = w
-                b = k * MID.npl + s * 6 + 1 + a
-                m_b[b, 8:16, :] = m_b[b, 8:16, :] + t[k, 0:8, :]
-            return carry
-
-        lax.fori_loop(0, 4, prolong1, 0)
-    exchange(MID, m_b, 7)
-    planes(MID, sweep(MID, "1", m_b, m_a, side_halo(MID, 7)))
-    exchange(MID, m_a, 8)
-    planes(MID, sweep(MID, "1", m_a, m_b, side_halo(MID, 8)))
-
-    for msg in a1:
-        msg.recv()
-    land_axial(FINE, ub, 1)
-    exchange(MID, m_b, 9)
-
-    def prolong0(q, carry):
+    def prolong1(sp, pp):
+        s, a = sp // 4, lax.rem(sp, 4)
+        xs = []
         for k in range(10):
-            w = m_b[k * MID.npl + zh * 6 + (q + 1) // 2]
-            t[k, pl.ds(0, 24, stride=2), :] = w
-            t[k, pl.ds(1, 24, stride=2), :] = w
-            ub[k * FINE.npl + q] = ub[k * FINE.npl + q] + t[k, 8:40, :]
-        return carry
-
-    lax.fori_loop(0, 10, prolong0, 0)
-    halo9 = side_halo(MID, 9)
-
-    def halo_up(k, sp):
-        w = halo9(k, zh * 4 + sp // 2)
+            w = q_a[k * COARSE.npl + s * 4 + 1 + a // 2, 8:16, :]
+            t[k, pl.ds(0, 8, stride=2), :] = w
+            t[k, pl.ds(1, 8, stride=2), :] = w
+            b = k * MID.npl + pp
+            xs.append(m_b[b, 8:16, :] + t[k, 0:8, :])
+            m_b[b, 8:16, :] = xs[k]
+        return xs
+
+    flying[7] = send(MID, m_b, 7, prolong1)
+    interior(MID, "1", m_b, m_a)
+    finish(MID, "1", m_a, 7, 8)
+    interior(MID, "1", m_a, m_b)
+    finish(MID, "1", m_b, 8, 9)
+
+    def double(k, w):
         t[k, pl.ds(0, 8, stride=2), :] = w
         t[k, pl.ds(1, 8, stride=2), :] = w
-        return halo1(k, sp) + t[k, 0:16, :]
-
-    planes(FINE, sweep(FINE, "0", ub, ua, halo_up))
-
+        return t[k, 0:16, :]
+
+    def prolong0(a, carry):
+        for k in range(10):
+            w = m_b[k * MID.npl + zh * 6 + 1 + a // 2, 8:16, :]
+            b = k * FINE.npl + 1 + a
+            ub[b, 8:24, :] = ub[b, 8:24, :] + double(k, w)
+        return carry
+
+    lax.fori_loop(0, 8, prolong0, 0)
+    interior(FINE, "0", ub, ua)
+    planes(FINE, lambda sp, pp: add(FINE, "0", ua, sp, pp, inplane(FINE, 1, sp)) and None)
+    recv(a1)
+    add_axial(FINE, "0", ua, 1)
+    a9, b9 = flying.pop(9)
+    recv(a9)
+    axr9 = v["axr_9"]
+    for end, a in ((0, 0), (1, 7)):
+        both = [split(axr9[2 * zh + end, k]) for k in range(5)]
+        h = [w[0] for w in both] + [w[1] for w in both]
+        add(FINE, "0", ua, a, a + 1, [double(k, h[k]) for k in range(10)])
+    recv(b9)
+    turn(MID, 9)
+    side9 = side_halo(MID, 9)
+
+    def add9(sp, pp):
+        am = zh * 4 + sp // 2
+        rows = row_halo(MID, 9, am)
+        return add(FINE, "0", ua, sp, pp, [ring(16, 1, double(k, side9(k, am)), *rows[k]) for k in range(10)])
+
+    planes(FINE, lambda sp, pp: add9(sp, pp) and None, 0, 8, 7)
     pack_axial(FINE, ua, 10)
     a10 = axial_msgs(FINE, 10)
     for msg in a10:
         msg.start()
+    planes(FINE, lambda sp, pp: add9(sp, pp) and None, 1, 7)
     pack_inplane(FINE, ua, 10)
     b10 = inplane_msgs(FINE, 10)
     for msg in b10:
         msg.start()
-    for msg in b10:
-        msg.recv()
-    land_inplane(FINE, ua, 10)
-    outv, mask = v["outv"], v["mask"]
-    halo10 = side_halo(FINE, 10)
+
+    mask = v["mask"]
+    interior(FINE, "0", ua, ub)
+    recv(b10)
+    turn(FINE, 10)
+
+    def work(a, new):
+        for k in range(10):
+            out[k * 8 + a] = new[k]
+        return mask[a].astype(F32) * (new[4] * new[6] - new[9] * new[1])
 
     def last(a, acc):
-        xs, res = residual(FINE, "0", ua, a, a + 1, halo10)
-        corr = smooth(FINE, "0", a, res)
-        new = [xs[k] + corr[k] for k in range(10)]
-        for k in range(10):
-            outv[k * 8 + a] = new[k]
-        return acc + mask[a].astype(F32) * (new[4] * new[6] - new[9] * new[1])
+        return acc + work(a, add(FINE, "0", ub, a, a + 1, inplane(FINE, 10, a)))
 
     acc = lax.fori_loop(1, 7, last, jnp.zeros((16, W), F32))
-    for msg in a10:
-        msg.recv()
-    land_axial(FINE, ua, 10)
-    acc = lax.fori_loop(0, 2, lambda i, c: last(7 * i, c), acc)
-    store = pltpu.make_async_copy(outv, out, v["ls"].at[8])
-    store.start()
+    planes(FINE, lambda sp, pp: add(FINE, "0", ub, sp, pp, inplane(FINE, 10, sp)) and None, 0, 8, 7)
+    recv(a10)
+    for end, a in ((0, 0), (1, 7)):
+        acc = acc + work(a, add(FINE, "0", ub, a, a + 1, beside(FINE, 10, end)))
 
     red0, red1 = v["red0"], v["red1"]
     mine0 = x * n_rad + rad
@@ -719,7 +756,6 @@
     for i in range(1, n1):
         total = total + red1[i]
     damp[0, 0] = jnp.sum(total) * (25.0 / jnp.sqrt(jnp.float32(cells)))
-    store.wait()
     for msg in sent:
         when(msg.send_if, msg.copy.wait_send)
 
@@ -733,21 +769,26 @@
         out, damp = pl.pallas_call(
             functools.partial(kernel, sizes + (cells,), tuple(shapes)),
             out_shape=(jax.ShapeDtypeStruct((80, 16, W), F32), jax.ShapeDtypeStruct((1, 1), F32)),
-            in_specs=[pl.BlockSpec(memory_space=pl.ANY)] * 8,
-            out_specs=(pl.BlockSpec(memory_space=pl.ANY), pl.BlockSpec(memory_space=pltpu.SMEM)),
+            in_specs=[pl.BlockSpec(memory_space=pltpu.HBM)] * 8,
+            out_specs=(pl.BlockSpec(memory_space=pltpu.VMEM), pl.BlockSpec(memory_space=pltpu.SMEM)),
             scratch_shapes=list(shapes.values()),
             compiler_params=pltpu.CompilerParams(
                 collective_id=0, has_side_effects=True, vmem_limit_bytes=48 * 1024 * 1024
             ),
         )(
-            rhs.reshape(80, 16, W),
-            jac0.reshape(200, 16, W),
-            shift0,
-            jac1.reshape(100, 8, 64),
-            shift1,
-            jac2.reshape(50, 4, 32),
-            shift2,
-            blade_mask,
+            *(
+                pltpu.with_memory_space_constraint(a, pltpu.HBM)
+                for a in (
+                    rhs.reshape(80, 16, W),
+                    jac0.reshape(200, 16, W),
+                    shift0,
+                    jac1.reshape(100, 8, 64),
+                    shift1,
+                    jac2.reshape(50, 4, 32),
+                    shift2,
+                    blade_mask,
+                )
+            )
         )
         return out.reshape(rhs.shape), damp.reshape(())
 

time: 121 us -> 96.8 us (0.80)
  Pallas kernels: 110 us -> 93.5 us
  local copies, waits for them, and re-layouts: 8.33 us -> 0.84 us
    pallas_call x1, Pallas kernels: 110 us -> 93.5 us  [on_device(): pl.pallas_call(functools.partial(kernel, sizes + (cells,), tuple(shapes))...]
    unnamed x17 -> x1, local copies, waits for them, and re-layouts: 8.33 us -> 0.84 us
where the time goes in v1:
time: 96.8 us; the launch traced here: 96.7 us
  Pallas kernels  93.5 us (97%)
  between operations  2.33 us (2%)
    pallas_call x1, Pallas kernels, on_device(): pl.pallas_call(functools.partial(kernel, sizes + (cells,), tuple(shapes))...  93.5 us

profile of v1, /device:TPU:1, one launch (start us, length us, event | category | flops | bytes accessed | tf_op | source)
XLA Modules:
  0.0 96.7 jit_solution(15494830403517642514)
XLA Ops:
  0.6 93.5 %shard_map.95 = (f32[80,16,128]{2,1,0:T(8,128)S(1)}, f32[1,1]{1,0:T(1,128)}) custom-call(f32[80,16,128]{2,1,0:T(8,128)} %bitcast.8, f32[200,16,128]{2,1,0:T(8,128)} %bitcast.7, f32[8,16,128]{2,1,0:T(8,128)} %refs_2_.1, f32[100,8,64]{2,1,0:T(8,128)} %bitcast.9, f32[4,8,64]{2,1,0:T(8,128)} %refs_4_.1, f32[50,4,32]{2,1,0:T(4,128)} %bitcast.10, ...), custom_call_target="tpu_custom_call" | custom-call | tf_op jit(solution)/shard_map/pallas_call | solution.py:769
  94.2 0.8 copy.12

commit v2 on v1

--- a/solution.py
+++ b/solution.py
@@ -45,6 +45,15 @@
 def split(w):
     even = (lanes(w.shape[0]) & 1) == 0
     return jnp.where(even, w, roll(w, 1)), jnp.where(even, roll(w, W - 1), w)
+
+
+def join2(a, b):
+    return jnp.where((lanes(a.shape[0]) & 2) == 0, a, b)
+
+
+def split2(w):
+    low = (lanes(w.shape[0]) & 2) == 0
+    return jnp.where(low, w, roll(w, 2)), jnp.where(low, roll(w, W - 2), w)
 
 
 def scratch():
@@ -78,8 +87,8 @@
     vmem("gr", 20, 8, W)
     vmem("c1s", 52, 8, W)
     vmem("c1r", 52, 8, W)
-    vmem("c2s", 13, 8, W)
-    vmem("c2r", 13, 8, W)
+    vmem("c2s", 7, 8, W)
+    vmem("c2r", 7, 8, W)
     vmem("t", 10, 48, W)
     vmem("j1", 104, 8, 64)
     vmem("j2", 52, 4, 32)
@@ -97,6 +106,7 @@
 ROUNDS = len(LEVEL_OF)
 COPIES = 128
 UNROLL = 2
+SPLIT = 8
 
 
 def kernel(sizes, names, *refs):
@@ -479,7 +489,6 @@
     for msg in b0:
         msg.start()
 
-    interior(FINE, "0", ua, ub)
     for c in loads[3:]:
         c.wait()
 
@@ -516,14 +525,18 @@
     for e in range(26):
         c2[e * 4 + zh * 2, 0:4, :] = y2[e, 0:4]
         c2[e * 4 + zh * 2 + 1, 0:4, :] = y2[e, 4:8]
-    for e in range(13):
-        c2s[e] = join(y2[e], y2[e + 13])
+    for e in range(7):
+        c2s[e] = join2(join(y2[e], y2[e + 7]), join(y2[e + 14], y2[min(e + 21, 25)]))
+    first_part, rest = pl.ds(0, SPLIT), pl.ds(SPLIT, 52 - SPLIT)
+    mc = [
+        Msg(c1s.at[first_part], c1r.at[first_part], twin),
+        Msg(c1s.at[rest], c1r.at[rest], twin),
+        Msg(c2s, c2r, twin),
+    ]
+    mc[0].start()
+    interior(FINE, "0", ua, ub)
 
     recv(b0)
-    mc1 = Msg(c1s, c1r, twin)
-    mc2 = Msg(c2s, c2r, twin)
-    mc1.start()
-    mc2.start()
     turn(FINE, 0)
     planes(FINE, lambda sp, pp: add(FINE, "0", ub, sp, pp, inplane(FINE, 0, sp)) and None)
     recv(a0)
@@ -546,6 +559,8 @@
     b1 = inplane_msgs(FINE, 1)
     for msg in b1:
         msg.start()
+    for msg in mc[1:]:
+        msg.start()
     f_part = v["f_part"]
 
     def restrict0(a, carry):
@@ -578,26 +593,24 @@
     mg = Msg(gs, gr, twin)
     mg.start()
     pack_axial(FINE, ub, 1)
-    a1 = axial_msgs(FINE, 1)
-    for msg in a1:
-        msg.start()
     for k in range(10):
         f1[pl.ds(k * 8 + zh * 4, 4)] = f_part[k * 4 : k * 4 + 4]
-    mc1.recv()
-    mc2.recv()
+    recv(mc)
 
     def split1(e, carry):
         for a in range(4):
             lo, hi = split(c1r[e * 4 + a])
             c1[e * 8 + (1 - zh) * 4 + a] = lo
             c1[(e + 13) * 8 + (1 - zh) * 4 + a] = hi
-        lo, hi = split(c2r[e])
-        for a in range(2):
-            c2[e * 4 + (1 - zh) * 2 + a, 0:4, :] = lo[4 * a : 4 * a + 4]
-            c2[(e + 13) * 4 + (1 - zh) * 2 + a, 0:4, :] = hi[4 * a : 4 * a + 4]
         return carry
 
-    lax.fori_loop(0, 13, split1, 0)
+    lax.fori_loop(0, 13, split1, 0, unroll=2)
+    for e in range(7):
+        low, high = split2(c2r[e])
+        for i, y in enumerate(split(low) + split(high)):
+            if e + 7 * i < 26:
+                for a in range(2):
+                    c2[(e + 7 * i) * 4 + (1 - zh) * 2 + a, 0:4, :] = y[4 * a : 4 * a + 4]
     coefficients(MID, "1")
     coefficients(COARSE, "2")
     mg.recv()
@@ -609,8 +622,20 @@
 
     m_a, m_b = v["ua1"], v["ub1"]
     flying[2] = send(MID, m_a, 2, first_plane(MID, "1", m_a))
+    axs1, axr1 = v["axs_1"], v["axr_1"]
+    a1 = []
+
+    def piece():
+        two = pl.ds(len(a1), 2)
+        for dst, dev, there, here in ((0, up, has_up, has_down), (1, down, has_down, has_up)):
+            msg = Msg(axs1.at[1 - dst, two], axr1.at[dst, two], dev, there, here)
+            msg.start()
+            a1.append(msg)
+
+    piece()
     interior(MID, "1", m_a, m_b)
     finish(MID, "1", m_b, 2, 3)
+    piece()
     f2 = v["f2"]
     for s in range(2):
 
@@ -637,6 +662,7 @@
     q_a, q_b = v["ua2"], v["ub2"]
     flying[4] = send(COARSE, q_a, 4, first_plane(COARSE, "2", q_a))
     for r in range(4, 3 + COARSE_SWEEPS):
+        piece()
         interior(COARSE, "2", q_a, q_b)
         finish(COARSE, "2", q_b, r, r + 1 if r < 2 + COARSE_SWEEPS else None)
         q_a, q_b = q_b, q_a
@@ -722,40 +748,40 @@
     for end, a in ((0, 0), (1, 7)):
         acc = acc + work(a, add(FINE, "0", ub, a, a + 1, beside(FINE, 10, end)))
 
-    red0, red1 = v["red0"], v["red1"]
-    mine0 = x * n_rad + rad
-    red0[mine0] = acc[0:8] + acc[8:16]
-    msgs = []
-    n0 = nx * n_rad
-    for off in range(1, n0):
-        to = lax.rem(mine0 + off, n0)
-        back = lax.rem(mine0 + n0 - off, n0)
-        msgs.append(
-            Msg(red0.at[mine0], red0.at[mine0], place(to // n_rad, lax.rem(to, n_rad), z, core), landing=red0.at[back])
-        )
-    for msg in msgs:
-        msg.start()
-    for msg in msgs:
-        msg.recv()
-    total = red0[0]
-    for i in range(1, n0):
-        total = total + red0[i]
-    mine1 = z * 2 + core
-    red1[mine1] = total
-    msgs = []
-    n1 = nz * 2
-    for off in range(1, n1):
-        to = lax.rem(mine1 + off, n1)
-        back = lax.rem(mine1 + n1 - off, n1)
-        msgs.append(Msg(red1.at[mine1], red1.at[mine1], place(x, rad, to // 2, lax.rem(to, 2)), landing=red1.at[back]))
-    for msg in msgs:
-        msg.start()
-    for msg in msgs:
-        msg.recv()
-    total = red1[0]
-    for i in range(1, n1):
-        total = total + red1[i]
-    damp[0, 0] = jnp.sum(total) * (25.0 / jnp.sqrt(jnp.float32(cells)))
+    def total(buf, group, value):
+        mine, count, members = group
+        buf[mine] = value
+        msgs = [Msg(buf.at[mine], buf.at[mine], dev, landing=buf.at[slot]) for dev, slot in members]
+        earlier = list(sent)
+        sent.clear()
+        for msg in msgs:
+            msg.start()
+        for msg in earlier:
+            when(msg.send_if, msg.copy.wait_send)
+        recv(msgs)
+        parts = [buf[i] for i in range(count)]
+        while len(parts) > 1:
+            parts = [p + q for p, q in zip(parts[::2], parts[1::2])] + parts[len(parts) - len(parts) % 2 :]
+        return parts[0]
+
+    def offsets(*counts):
+        far = lambda o: sum(min(d, n - d) for d, n in zip(o, counts))
+        every = [(i, j) for i in range(counts[0]) for j in range(counts[1])]
+        return sorted(every[1:], key=lambda o: -far(o))
+
+    across = []
+    for i, j in offsets(nx, n_rad):
+        there = lambda sign: (lax.rem(x + sign * i + nx, nx), lax.rem(rad + sign * j + n_rad, n_rad))
+        (tx, ty), (fx, fy) = there(1), there(-1)
+        across.append((place(tx, ty, z, core), fx * n_rad + fy))
+    along = []
+    for i, j in offsets(nz, 2):
+        tz, fz = lax.rem(z + i, nz), lax.rem(z + nz - i, nz)
+        other = core if j == 0 else 1 - core
+        along.append((place(x, rad, tz, other), fz * 2 + other))
+    sum_xy = total(v["red0"], (x * n_rad + rad, nx * n_rad, across), acc[0:8] + acc[8:16])
+    sum_all = total(v["red1"], (z * 2 + core, nz * 2, along), sum_xy)
+    damp[0, 0] = jnp.sum(sum_all) * (25.0 / jnp.sqrt(jnp.float32(cells)))
     for msg in sent:
         when(msg.send_if, msg.copy.wait_send)
 

time: 96.8 us -> 91.2 us (0.942)
  Pallas kernels: 93.5 us -> 88 us
    pallas_call x1, Pallas kernels: 93.5 us -> 88 us  [on_device(): pl.pallas_call(functools.partial(kernel, sizes + (cells,), tuple(shapes))...]
where the time goes in v2:
time: 91.2 us; the launch traced here: 91.1 us
  Pallas kernels  88 us (96%)
  between operations  2.33 us (3%)
    pallas_call x1, Pallas kernels, on_device(): pl.pallas_call(functools.partial(kernel, sizes + (cells,), tuple(shapes))...  88 us

profile of v2, /device:TPU:1, one launch (start us, length us, event | category | flops | bytes accessed | tf_op | source)
XLA Modules:
  0.0 91.1 jit_solution(14011261566855881180)
XLA Ops:
  0.6 88.0 %shard_map.95 = (f32[80,16,128]{2,1,0:T(8,128)S(1)}, f32[1,1]{1,0:T(1,128)}) custom-call(f32[80,16,128]{2,1,0:T(8,128)} %bitcast.8, f32[200,16,128]{2,1,0:T(8,128)} %bitcast.7, f32[8,16,128]{2,1,0:T(8,128)} %refs_2_.1, f32[100,8,64]{2,1,0:T(8,128)} %bitcast.9, f32[4,8,64]{2,1,0:T(8,128)} %refs_4_.1, f32[50,4,32]{2,1,0:T(4,128)} %bitcast.10, ...), custom_call_target="tpu_custom_call" | custom-call | tf_op jit(solution)/shard_map/pallas_call | solution.py:795
  88.6 0.8 copy.12

commit v3 on v2

--- a/solution.py
+++ b/solution.py
@@ -98,15 +98,15 @@
     shapes["mask"] = pltpu.VMEM((8, 16, W), jnp.int32)
     shapes["ss"] = pltpu.SemaphoreType.DMA((COPIES,))
     shapes["rs"] = pltpu.SemaphoreType.DMA((COPIES,))
-    shapes["ls"] = pltpu.SemaphoreType.DMA((10,))
+    shapes["ls"] = pltpu.SemaphoreType.DMA((16,))
     return shapes
 
 
 LEVEL_OF = [FINE, FINE, MID, MID, COARSE, COARSE, COARSE, MID, MID, MID, FINE]
 ROUNDS = len(LEVEL_OF)
 COPIES = 128
-UNROLL = 2
-SPLIT = 8
+UNROLL = 4
+SPLIT = 20
 
 
 def kernel(sizes, names, *refs):
@@ -147,8 +147,9 @@
 
     local = [
         (rhs, v["f0"]),
-        (jac0, v["c0"].at[pl.ds(0, 200)]),
         (shift0, v["c0"].at[pl.ds(200, 8)]),
+        *((jac0.at[pl.ds(48 * i, 8)], v["c0"].at[pl.ds(48 * i, 8)]) for i in range(5)),
+        *((jac0.at[pl.ds(48 * i + 8, 40)], v["c0"].at[pl.ds(48 * i + 8, 40)]) for i in range(4)),
         (jac1, v["j1"].at[pl.ds(0, 100)]),
         (shift1, v["j1"].at[pl.ds(100, 4)]),
         (jac2, v["j2"].at[pl.ds(0, 50)]),
@@ -464,16 +465,7 @@
     ua, ub = v["ua0"], v["ub0"]
     f1, c1, c2 = v["f1"], v["c1"], v["c2"]
 
-    for tag, lv in (("0", FINE), ("1", MID), ("2", COARSE)):
-        for u in (v["ua" + tag], v["ub" + tag]):
-
-            def clear(i, carry, u=u, lv=lv):
-                u[i] = jnp.zeros((lv.height, W), F32)
-                return carry
-
-            lax.fori_loop(0, 10 * lv.npl, clear, 0)
-
-    for c in loads[:3]:
+    for c in loads[:7]:
         c.wait()
     coefficients(FINE, "0")
     first(FINE, "0", ua)
@@ -489,7 +481,22 @@
     for msg in b0:
         msg.start()
 
-    for c in loads[3:]:
+    for tag, lv in (("0", FINE), ("1", MID), ("2", COARSE)):
+        for u in (v["ua" + tag], v["ub" + tag]):
+
+            def clear(k, carry, u=u, lv=lv):
+                for q in range(lv.npl):
+                    i = k * lv.npl + q
+                    if q % lv.pad in (0, lv.pad - 1):
+                        u[i] = jnp.zeros((lv.height, W), F32)
+                    else:
+                        u[i, 0:8, :] = jnp.zeros((8, W), F32)
+                        u[i, 8 + lv.nr : lv.height, :] = jnp.zeros((lv.height - 8 - lv.nr, W), F32)
+                return carry
+
+            lax.fori_loop(0, 10, clear, 0)
+
+    for c in loads[7:]:
         c.wait()
 
     def spread(cells_in):
@@ -533,10 +540,10 @@
         Msg(c1s.at[rest], c1r.at[rest], twin),
         Msg(c2s, c2r, twin),
     ]
+    interior(FINE, "0", ua, ub)
+
+    recv(b0)
     mc[0].start()
-    interior(FINE, "0", ua, ub)
-
-    recv(b0)
     turn(FINE, 0)
     planes(FINE, lambda sp, pp: add(FINE, "0", ub, sp, pp, inplane(FINE, 0, sp)) and None)
     recv(a0)
@@ -581,17 +588,23 @@
         return carry
 
     lax.fori_loop(0, 4, restrict_halo0, 0)
+    gs, gr = v["gs"], v["gr"]
+    order = (1, 2, 0, 3)
+    mg = [Msg(gs.at[half], gr.at[half], twin) for half in (pl.ds(0, 10), pl.ds(10, 10))]
+    for i in range(10):
+        k, a = i % 5, order[i // 5]
+        gs[i] = join(f_part[k * 4 + a], f_part[(5 + k) * 4 + a])
+    mg[0].start()
     recv(parts)
-    gs, gr = v["gs"], v["gr"]
     for k in range(5):
         for end, a in ((0, 0), (1, 3)):
             re, im = split(part_r[end, k])
             f_part[k * 4 + a] = f_part[k * 4 + a] + 0.125 * re
             f_part[(5 + k) * 4 + a] = f_part[(5 + k) * 4 + a] + 0.125 * im
-    for i in range(20):
-        gs[i] = join(f_part[i], f_part[20 + i])
-    mg = Msg(gs, gr, twin)
-    mg.start()
+    for i in range(10, 20):
+        k, a = i % 5, order[i // 5]
+        gs[i] = join(f_part[k * 4 + a], f_part[(5 + k) * 4 + a])
+    mg[1].start()
     pack_axial(FINE, ub, 1)
     for k in range(10):
         f1[pl.ds(k * 8 + zh * 4, 4)] = f_part[k * 4 : k * 4 + 4]
@@ -613,10 +626,10 @@
                     c2[(e + 7 * i) * 4 + (1 - zh) * 2 + a, 0:4, :] = y[4 * a : 4 * a + 4]
     coefficients(MID, "1")
     coefficients(COARSE, "2")
-    mg.recv()
+    recv(mg)
     for i in range(20):
         re, im = split(gr[i])
-        k, a = i // 4, i % 4
+        k, a = i % 5, order[i // 5]
         f1[k * 8 + (1 - zh) * 4 + a] = re
         f1[(k + 5) * 8 + (1 - zh) * 4 + a] = im
 
@@ -750,8 +763,11 @@
 
     def total(buf, group, value):
         mine, count, members = group
-        buf[mine] = value
-        msgs = [Msg(buf.at[mine], buf.at[mine], dev, landing=buf.at[slot]) for dev, slot in members]
+        buf[mine, 0:1] = value
+        row = pl.ds(0, 1)
+        msgs = [
+            Msg(buf.at[mine, row], buf.at[mine, row], dev, landing=buf.at[slot, row]) for dev, slot in members
+        ]
         earlier = list(sent)
         sent.clear()
         for msg in msgs:
@@ -759,7 +775,7 @@
         for msg in earlier:
             when(msg.send_if, msg.copy.wait_send)
         recv(msgs)
-        parts = [buf[i] for i in range(count)]
+        parts = [buf[i, 0:1] for i in range(count)]
         while len(parts) > 1:
             parts = [p + q for p, q in zip(parts[::2], parts[1::2])] + parts[len(parts) - len(parts) % 2 :]
         return parts[0]
@@ -779,7 +795,7 @@
         tz, fz = lax.rem(z + i, nz), lax.rem(z + nz - i, nz)
         other = core if j == 0 else 1 - core
         along.append((place(x, rad, tz, other), fz * 2 + other))
-    sum_xy = total(v["red0"], (x * n_rad + rad, nx * n_rad, across), acc[0:8] + acc[8:16])
+    sum_xy = total(v["red0"], (x * n_rad + rad, nx * n_rad, across), jnp.sum(acc, axis=0, keepdims=True))
     sum_all = total(v["red1"], (z * 2 + core, nz * 2, along), sum_xy)
     damp[0, 0] = jnp.sum(sum_all) * (25.0 / jnp.sqrt(jnp.float32(cells)))
     for msg in sent:

time: 91.2 us -> 90.4 us (level)
  no operation moved by 1% of the time
where the time goes in v3:
time: 90.4 us; the launch traced here: 90.2 us
  Pallas kernels  87.1 us (96%)
  between operations  2.33 us (3%)
    pallas_call x1, Pallas kernels, on_device(): pl.pallas_call(functools.partial(kernel, sizes + (cells,), tuple(shapes))...  87.1 us

profile of v3, /device:TPU:1, one launch (start us, length us, event | category | flops | bytes accessed | tf_op | source)
XLA Modules:
  0.0 90.2 jit_solution(11032806395801160523)
XLA Ops:
  0.6 87.1 %shard_map.95 = (f32[80,16,128]{2,1,0:T(8,128)S(1)}, f32[1,1]{1,0:T(1,128)}) custom-call(f32[80,16,128]{2,1,0:T(8,128)} %bitcast.8, f32[200,16,128]{2,1,0:T(8,128)} %bitcast.7, f32[8,16,128]{2,1,0:T(8,128)} %refs_2_.1, f32[100,8,64]{2,1,0:T(8,128)} %bitcast.9, f32[4,8,64]{2,1,0:T(8,128)} %refs_4_.1, f32[50,4,32]{2,1,0:T(4,128)} %bitcast.10, ...), custom_call_target="tpu_custom_call" | custom-call | tf_op jit(solution)/shard_map/pallas_call | solution.py:811
  87.7 0.8 copy.12

commit v4 on v3

--- a/solution.py
+++ b/solution.py
@@ -145,21 +145,6 @@
         else:
             pl.when(cond)(act)
 
-    local = [
-        (rhs, v["f0"]),
-        (shift0, v["c0"].at[pl.ds(200, 8)]),
-        *((jac0.at[pl.ds(48 * i, 8)], v["c0"].at[pl.ds(48 * i, 8)]) for i in range(5)),
-        *((jac0.at[pl.ds(48 * i + 8, 40)], v["c0"].at[pl.ds(48 * i + 8, 40)]) for i in range(4)),
-        (jac1, v["j1"].at[pl.ds(0, 100)]),
-        (shift1, v["j1"].at[pl.ds(100, 4)]),
-        (jac2, v["j2"].at[pl.ds(0, 50)]),
-        (shift2, v["j2"].at[pl.ds(50, 2)]),
-        (blade, v["mask"]),
-    ]
-    loads = [pltpu.make_async_copy(a, b, v["ls"].at[i]) for i, (a, b) in enumerate(local)]
-    for c in loads:
-        c.start()
-
     barrier = pltpu.get_barrier_semaphore()
     greet = [
         (up, has_up),
@@ -175,6 +160,21 @@
     ]
     for dev, cond in greet:
         when(cond, lambda dev=dev: pl.semaphore_signal(barrier, inc=1, device_id=dev, device_id_type=MESH))
+
+    local = [
+        (rhs, v["f0"]),
+        (shift0, v["c0"].at[pl.ds(200, 8)]),
+        *((jac0.at[pl.ds(48 * i, 8)], v["c0"].at[pl.ds(48 * i, 8)]) for i in range(5)),
+        *((jac0.at[pl.ds(48 * i + 8, 40)], v["c0"].at[pl.ds(48 * i + 8, 40)]) for i in range(4)),
+        (jac1, v["j1"].at[pl.ds(0, 100)]),
+        (shift1, v["j1"].at[pl.ds(100, 4)]),
+        (jac2, v["j2"].at[pl.ds(0, 50)]),
+        (shift2, v["j2"].at[pl.ds(50, 2)]),
+        (blade, v["mask"]),
+    ]
+    loads = [pltpu.make_async_copy(a, b, v["ls"].at[i]) for i, (a, b) in enumerate(local)]
+    for c in loads:
+        c.start()
 
     counter = [0]
     sent = []

time: 90.4 us -> 89.5 us (0.990)
  no operation moved by 1% of the time
where the time goes in v4:
time: 89.5 us; the launch traced here: 89.4 us
  Pallas kernels  86.2 us (96%)
  between operations  2.33 us (3%)
    pallas_call x1, Pallas kernels, on_device(): pl.pallas_call(functools.partial(kernel, sizes + (cells,), tuple(shapes))...  86.2 us

profile of v4, /device:TPU:1, one launch (start us, length us, event | category | flops | bytes accessed | tf_op | source)
XLA Modules:
  0.0 89.4 jit_solution(4544892172142605747)
XLA Ops:
  0.6 86.2 %shard_map.95 = (f32[80,16,128]{2,1,0:T(8,128)S(1)}, f32[1,1]{1,0:T(1,128)}) custom-call(f32[80,16,128]{2,1,0:T(8,128)} %bitcast.8, f32[200,16,128]{2,1,0:T(8,128)} %bitcast.7, f32[8,16,128]{2,1,0:T(8,128)} %refs_2_.1, f32[100,8,64]{2,1,0:T(8,128)} %bitcast.9, f32[4,8,64]{2,1,0:T(8,128)} %refs_4_.1, f32[50,4,32]{2,1,0:T(4,128)} %bitcast.10, ...), custom_call_target="tpu_custom_call" | custom-call | tf_op jit(solution)/shard_map/pallas_call | solution.py:811
  86.8 0.8 copy.12
